TPU v7x, 32 devices: a whole 2x2x4 slice. The times are simulated.
32 devices in a mesh: space: 8 (over z, y), chan: 4 (over x, core).
Axes of the slice: x: 2, y: 2, z: 4, core: 2. Of those that a mesh axis runs over, the one named last changes fastest.
Arguments:
- features: bfloat16 [128, 64, 128], P('space'), may hold values from -6 to 6
- neighbours: int32 [128, 26], P('space'), may hold values from -1 to 127, as said below
- parent_index: int32 [128], P('space'), may hold values from 0 to 31, as said below
- octant: int32 [128], P('space'), may hold values from 0 to 7, as said below
- parent_dest: int32 [32], P('space'), may hold values from 0 to 63, as said below
- conv_fine: bfloat16 [128, 3456], P('chan'), may hold values from -0.109375 to 0.109375
- conv_down: bfloat16 [256, 3456], P('chan'), may hold values from -0.15625 to 0.15625
- conv_coarse: bfloat16 [256, 6912], P('chan'), may hold values from -0.15625 to 0.15625
- norm_gain: float32 [256], P('chan'), may hold values from 0.25 to 1.75
Outputs:
- coarse_parents: bfloat16 [256, 4096], P('chan', 'space')
Inputs may be any that keep to these rules, and one draw needn't show every extreme that they name: Brick n lies on device n // 16 of space. Device d holds 16 distinct positions of a slab of 2 x 4 x 4 brick positions (x = 2 d or 2 d + 1, y, z); brick n's position gives parent_index[n] = d * 4 + (y // 2) * 2 + z // 2 and octant[n] = x % 2 + 2 (y % 2) + 4 (z % 2). neighbours[n, k] is the brick at the k-th offset (a, b, c), a, b, c in -1, 0, 1, (0, 0, 0) left out, in increasing 9 a + 3 b + c, or -1 where that position holds no brick. `parent_index`: as stated for neighbours. `octant`: as stated for neighbours. parent_dest[g] = owner * 8 + slot, where the owner of a parent of device d is d - 1, d or d + 1. At most 2 parents of one device go to each of its two neighbours, and some device sends 2 to a neighbour; some owner receives 8 parents. An owner's slots are filled from 0 upward without gaps, in order of source device and then of parent.
All inputs are finite; a program needn't handle non-finite values.
Results may differ from a plain program's by a relative error of at most 0.0065.
Values may be sent and summed in bfloat16 or wider, within the bound.
A program may use at most 64 MiB of HBM per device.

v0:
```python
import jax
import jax.numpy as jnp
from jax import lax
from jax.sharding import PartitionSpec as P

COARSE_CH = 256
EDGE = 4
SLAB_Y = 4
SLAB_Z = 4
PARENT_DEV = 4


offset_list = [(a, b, c) for a in (-1, 0, 1) for b in (-1, 0, 1) for c in (-1, 0, 1)]
around_list = [item for item in offset_list if item != (0, 0, 0)]
epsilon = 1e-06


def passed_along(value, axis, steps):
    count = lax.axis_size(axis)
    first, last = (max(0, -steps), min(count, count - steps))
    return lax.ppermute(value, axis, [(source, source + steps) for source in range(first, last)])


def extended(block, sides, width):
    for axis, dim in sides:
        count = lax.axis_size(axis)
        forward = [(i, i + 1) for i in range(count - 1)]
        backward = [(target, source) for source, target in forward]
        low = lax.ppermute(
            lax.slice_in_dim(block, block.shape[dim] - width, None, axis=dim), axis, forward
        )
        high = lax.ppermute(lax.slice_in_dim(block, 0, width, axis=dim), axis, backward)
        block = jnp.concatenate([low, block, high], axis=dim)
    return block


def stride_span(first, number, stride):
    return slice(first, first + stride * (number - 1) + 1, stride)


def source_span(offset, length):
    if offset < 0:
        return slice(length - 1, length)
    if offset == 0:
        return slice(0, length)
    return slice(0, 1)


def apply_taps(padded, weight, counts, stride):
    in_width = padded.shape[-1]
    accumulated = None
    for t, (a, b, c) in enumerate(offset_list):
        window = padded[
            :,
            stride_span(1 + a, counts[0], stride),
            stride_span(1 + b, counts[1], stride),
            stride_span(1 + c, counts[2], stride),
        ]
        tap_block = weight[:, t * in_width : (t + 1) * in_width]
        product = lax.dot_general(
            window.reshape(-1, in_width),
            tap_block,
            (((1,), (1,)), ((), ())),
            preferred_element_type=jnp.float32,
        )
        accumulated = product if accumulated is None else accumulated + product
    return accumulated.reshape((padded.shape[0],) + tuple(counts) + (weight.shape[0],))


def surround(bricks, from_left, from_right, link_rows, device, lower_only):
    brick_count = bricks.shape[0]
    length = bricks.shape[1]
    blank_row = jnp.zeros((1,) + bricks.shape[1:], bricks.dtype)
    owner_dev = link_rows // brick_count
    within = link_rows % brick_count
    middle = jnp.concatenate([bricks, blank_row], 0)
    lower_pool = jnp.concatenate([bricks[:, length - 1 : length], from_left, blank_row[:, :1]], 0)
    upper_pool = None
    if not lower_only:
        upper_pool = jnp.concatenate([bricks[:, 0:1], from_right, blank_row[:, :1]], 0)
    spans = (-1, 0) if lower_only else (-1, 0, 1)
    layers = []
    for a in spans:
        rows_y = []
        for b in spans:
            cells_z = []
            for c in spans:
                if (a, b, c) == (0, 0, 0):
                    fragment = bricks
                else:
                    k = around_list.index((a, b, c))
                    present = link_rows[:, k] >= 0
                    is_local = present & (owner_dev[:, k] == device)
                    if a == 0:
                        source = middle
                        row_index = jnp.where(is_local, within[:, k], brick_count)
                    else:
                        source = lower_pool if a < 0 else upper_pool
                        row_index = jnp.where(
                            is_local,
                            within[:, k],
                            jnp.where(present, brick_count + within[:, k], 2 * brick_count),
                        )
                    trimmed = source[:, :, source_span(b, length), source_span(c, length)]
                    fragment = jnp.take(trimmed, row_index, axis=0)
                cells_z.append(fragment)
            rows_y.append(jnp.concatenate(cells_z, 3))
        layers.append(jnp.concatenate(rows_y, 2))
    return jnp.concatenate(layers, 1)


def assemble_slab(pieces, local_parent, octant):
    brick_count = pieces.shape[0]
    half_edge = pieces.shape[1]
    places = 2 * SLAB_Y * SLAB_Z
    x_bit = octant % 2
    y_pos = 2 * (local_parent // (SLAB_Z // 2)) + octant // 2 % 2
    z_pos = 2 * (local_parent % (SLAB_Z // 2)) + octant // 4
    position = x_bit + 2 * y_pos + 2 * SLAB_Y * z_pos
    matches = position[None, :] == jnp.arange(places, dtype=jnp.int32)[:, None]
    brick_ids = jnp.arange(brick_count, dtype=jnp.int32)
    row_index = jnp.where(
        jnp.any(matches, 1), jnp.sum(jnp.where(matches, brick_ids[None, :], 0), 1), brick_count
    )
    blank_row = jnp.zeros((1,) + pieces.shape[1:], pieces.dtype)
    placed = jnp.take(jnp.concatenate([pieces, blank_row], 0), row_index, axis=0)
    placed = placed.reshape(SLAB_Z, SLAB_Y, 2, half_edge, half_edge, half_edge, pieces.shape[-1])
    placed = placed.transpose(2, 3, 1, 4, 0, 5, 6)
    return placed.reshape(2 * half_edge, SLAB_Y * half_edge, SLAB_Z * half_edge, pieces.shape[-1])


def split_parents(coarse_slab):
    edge_cells = coarse_slab.shape[0]
    rows_y = coarse_slab.shape[1] // edge_cells
    rows_z = coarse_slab.shape[2] // edge_cells
    shaped = coarse_slab.reshape(
        edge_cells, rows_y, edge_cells, rows_z, edge_cells, coarse_slab.shape[-1]
    )
    shaped = shaped.transpose(1, 3, 0, 2, 4, 5)
    return shaped.reshape(rows_y * rows_z, edge_cells**3, coarse_slab.shape[-1])


def rescale(values, cell_power, norm_gain):
    return (values * lax.rsqrt(cell_power[..., None] / COARSE_CH + epsilon) * norm_gain).astype(
        jnp.bfloat16
    )


def outgoing_rows(flat_rows, owner_dev, slot_ids, target, capacity):
    parent_count = flat_rows.shape[0]
    order_ids = jnp.arange(parent_count, dtype=jnp.int32)
    chosen = owner_dev == target
    rank_ids = jnp.sum(chosen[None, :] & (order_ids[None, :] < order_ids[:, None]), 1)
    matches = chosen[None, :] & (
        rank_ids[None, :] == jnp.arange(capacity, dtype=jnp.int32)[:, None]
    )
    filled = jnp.any(matches, 1)
    row_index = jnp.where(
        filled, jnp.sum(jnp.where(matches, order_ids[None, :], 0), 1), parent_count
    )
    blank_row = jnp.zeros((1, flat_rows.shape[1]), flat_rows.dtype)
    rows_out = jnp.take(jnp.concatenate([flat_rows, blank_row], 0), row_index, axis=0)
    labels = jnp.where(filled, jnp.sum(jnp.where(matches, slot_ids[None, :] + 1, 0), 1), 0)
    return (rows_out, labels.astype(jnp.bfloat16))


def repack(parents, parent_dest):
    device = lax.axis_index("space")
    parent_count = parents.shape[0]
    capacity = parent_count // 2
    slots_dev = parent_count + 2 * capacity
    flat_rows = parents.reshape(parent_count, -1)
    owner_dev = parent_dest // slots_dev
    slot_ids = parent_dest % slots_dev
    upward_rows, upward_labels = outgoing_rows(flat_rows, owner_dev, slot_ids, device + 1, capacity)
    downward_rows, downward_labels = outgoing_rows(
        flat_rows, owner_dev, slot_ids, device - 1, capacity
    )
    from_lower, lower_labels = passed_along((upward_rows, upward_labels), "space", 1)
    from_upper, upper_labels = passed_along((downward_rows, downward_labels), "space", -1)
    own_tags = jnp.where(owner_dev == device, slot_ids, -1).astype(jnp.float32)
    tags = jnp.concatenate(
        [own_tags, lower_labels.astype(jnp.float32) - 1.0, upper_labels.astype(jnp.float32) - 1.0],
        0,
    )
    blank_row = jnp.zeros((1, flat_rows.shape[1]), flat_rows.dtype)
    stacked = jnp.concatenate([flat_rows, from_lower, from_upper, blank_row], 0)
    source_count = tags.shape[0]
    wanted = tags[None, :] == jnp.arange(slots_dev, dtype=jnp.float32)[:, None]
    source_ids = jnp.arange(source_count, dtype=jnp.int32)
    pick_index = jnp.where(
        jnp.any(wanted, 1), jnp.sum(jnp.where(wanted, source_ids[None, :], 0), 1), source_count
    )
    return jnp.take(stacked, pick_index, axis=0).reshape(
        slots_dev, parents.shape[1], parents.shape[2]
    )


def body(
    features,
    neighbours,
    parent_index,
    octant,
    parent_dest,
    conv_fine,
    conv_down,
    conv_coarse,
    norm_gain,
):
    brick_count = features.shape[0]
    half_edge = EDGE // 2
    device = lax.axis_index("space")
    bricks = features.reshape(brick_count, EDGE, EDGE, EDGE, features.shape[-1])
    from_left = passed_along(bricks[:, EDGE - 1 : EDGE], "space", 1)
    from_right = passed_along(bricks[:, 0:1], "space", -1)
    padded = surround(bricks, from_left, from_right, neighbours, device, False)
    hidden = jnp.maximum(apply_taps(padded, conv_fine, (EDGE, EDGE, EDGE), 1), 0.0).astype(
        jnp.bfloat16
    )
    widened = lax.all_gather(hidden, "chan", axis=4, tiled=True)
    rim_left = passed_along(widened[:, EDGE - 1 : EDGE], "space", 1)
    lowered = surround(widened, rim_left, None, neighbours, device, True)
    pieces = jnp.maximum(
        apply_taps(lowered, conv_down, (half_edge, half_edge, half_edge), 2), 0.0
    ).astype(jnp.bfloat16)
    coarse_slab = assemble_slab(pieces, parent_index - device * PARENT_DEV, octant)
    full_slab = lax.all_gather(coarse_slab, "chan", axis=3, tiled=True)
    framed = extended(full_slab, (("space", 0),), 1)
    span_y = coarse_slab.shape[1]
    span_z = coarse_slab.shape[2]
    framed = jnp.pad(framed, ((0, 0), (1, 1), (1, 1), (0, 0)))
    convolved = apply_taps(framed[None], conv_coarse, (EDGE, span_y, span_z), 1)[0].astype(
        jnp.bfloat16
    )
    parents = split_parents(convolved)
    received = repack(parents, parent_dest)
    values = received.astype(jnp.float32)
    cell_power = lax.psum(jnp.sum(values * values, -1), "chan")
    result = rescale(values, cell_power, norm_gain)
    return result.transpose(2, 0, 1).reshape(result.shape[2], result.shape[0] * result.shape[1])


def solution(mesh):
    return jax.shard_map(
        body,
        mesh=mesh,
        in_specs=(
            P("space", None, None),
            P("space", None),
            P("space"),
            P("space"),
            P("space"),
            P("chan", None),
            P("chan", None),
            P("chan", None),
            P("chan"),
        ),
        out_specs=P("chan", "space"),
        check_vma=False,
    )
```

profile of v0, /device:TPU:0, one launch (start us, length us, event | category | flops | bytes accessed | tf_op | source)
XLA Modules:
  0.0 829.8 jit_solution(3898791215307152194)
XLA Ops:
  0.0 1.1 copy.473
  1.2 1.3 collective-permute-start.3
  2.5 5.5 collective-permute-start.2
  9.3 1.3 collective-permute-start.1
  10.6 5.4 collective-permute-start
  17.6 1.2 fusion.89
  59.4 2.0 gather_fusion.27
  61.4 1.3 bitcast_select_fusion.25
  62.7 2.1 gather_fusion.26
  64.8 1.4 bitcast_select_fusion.12
  66.2 2.0 gather_fusion.25
  68.2 1.4 bitcast_select_fusion.26
  69.5 2.1 gather_fusion.24
  71.6 1.4 bitcast_select_fusion.13
  73.0 1.4 gather_fusion.23
  74.3 0.9 bitcast_select_fusion.3
  75.3 1.5 gather_fusion.22
  77.4 1.4 gather_fusion.21
  79.5 1.5 gather_fusion.20
  83.1 1.1 maximum_maximum_fusion.1
  91.5 0.9 copy.537
  92.4 15.9 %all_gather.6 = bf16[16,4,4,4,128]{0,3,2,1,4:T(4,128)(2,1)S(1)} all-gather(bf16[16,4,4,4,32]{0,3,2,1,4:T(4,128)(2,1)S(1)} %copy.537), channel_id=1, replica_groups=mesh['space'=8,'chan'=4] {'chan'}, dimensions={4}, use_global_device_ids=true | all-gather | bytes 327680 | tf_op jit(solution)/shard_map/all_gather | solution.py:220
  108.3 1.9 copy.538
  110.2 2.4 copy.545
  116.2 5.4 collective-permute-start.4
  123.0 143.1 %slice.1084 = bf16[16,2,2,2,128]{0,3,2,1,4:T(2,128)(2,1)} slice(bf16[16,4,4,4,128]{0,3,2,1,4:T(4,128)(2,1)S(1)} %all_gather.6), slice={[0:16:1], [0:3:2], [0:3:2], [0:3:2], [0:128:1]} | slice | bytes 65536 | tf_op jit(solution)/shard_map/slice | solution.py:53
  266.1 143.0 %slice.1086 = bf16[16,2,2,2,128]{0,3,2,1,4:T(2,128)(2,1)} slice(bf16[16,4,4,4,128]{0,3,2,1,4:T(4,128)(2,1)S(1)} %all_gather.6), slice={[0:16:1], [0:3:2], [0:3:2], [1:4:2], [0:128:1]} | slice | bytes 65536 | tf_op jit(solution)/shard_map/slice | solution.py:53
  409.1 143.1 %slice.1090 = bf16[16,2,2,2,128]{0,3,2,1,4:T(2,128)(2,1)} slice(bf16[16,4,4,4,128]{0,3,2,1,4:T(4,128)(2,1)S(1)} %all_gather.6), slice={[0:16:1], [0:3:2], [1:4:2], [0:3:2], [0:128:1]} | slice | bytes 65536 | tf_op jit(solution)/shard_map/slice | solution.py:53
  552.2 143.1 %slice.1092 = bf16[16,2,2,2,128]{0,3,2,1,4:T(2,128)(2,1)} slice(bf16[16,4,4,4,128]{0,3,2,1,4:T(4,128)(2,1)S(1)} %all_gather.6), slice={[0:16:1], [0:3:2], [1:4:2], [1:4:2], [0:128:1]} | slice | bytes 65536 | tf_op jit(solution)/shard_map/slice | solution.py:53
  695.3 12.1 %slice.1102 = bf16[16,2,2,2,128]{0,3,2,1,4:T(2,128)(2,1)S(1)} slice(bf16[16,4,4,4,128]{0,3,2,1,4:T(4,128)(2,1)S(1)} %all_gather.6), slice={[0:16:1], [1:4:2], [0:3:2], [0:3:2], [0:128:1]} | slice | bytes 65536 | tf_op jit(solution)/shard_map/slice | solution.py:53
  707.5 12.2 %slice.1104 = bf16[16,2,2,2,128]{0,3,2,1,4:T(2,128)(2,1)S(1)} slice(bf16[16,4,4,4,128]{0,3,2,1,4:T(4,128)(2,1)S(1)} %all_gather.6), slice={[0:16:1], [1:4:2], [0:3:2], [1:4:2], [0:128:1]} | slice | bytes 65536 | tf_op jit(solution)/shard_map/slice | solution.py:53
  719.7 19.0 %slice.1108 = bf16[16,2,2,2,128]{0,3,2,1,4:T(2,128)(2,1)S(1)} slice(bf16[16,4,4,4,128]{0,3,2,1,4:T(4,128)(2,1)S(1)} %all_gather.6), slice={[0:16:1], [1:4:2], [1:4:2], [0:3:2], [0:128:1]} | slice | bytes 65536 | tf_op jit(solution)/shard_map/slice | solution.py:53
  738.7 19.0 %slice.1110 = bf16[16,2,2,2,128]{0,3,2,1,4:T(2,128)(2,1)S(1)} slice(bf16[16,4,4,4,128]{0,3,2,1,4:T(4,128)(2,1)S(1)} %all_gather.6), slice={[0:16:1], [1:4:2], [1:4:2], [1:4:2], [0:128:1]} | slice | bytes 65536 | tf_op jit(solution)/shard_map/slice | solution.py:53
  760.9 1.1 copy.566
  762.1 1.1 copy.567
  764.0 1.1 copy.569
  765.2 1.1 copy.570
  770.2 1.0 maximum_maximum_fusion.8
  771.3 0.9 gather_fusion.31
  781.4 15.6 %all_gather.7 = bf16[4,8,8,256]{2,1,0,3:T(8,128)(2,1)S(1)} all-gather(bf16[4,8,8,64]{2,1,0,3:T(8,128)(2,1)S(1)} %copy.582), channel_id=1, replica_groups=mesh['space'=8,'chan'=4] {'chan'}, dimensions={3}, use_global_device_ids=true | all-gather | bytes 163840 | tf_op jit(solution)/shard_map/all_gather | solution.py:227
  797.0 1.6 copy.583
  798.7 1.3 collective-permute-start.6
  800.0 4.5 collective-permute-start.5
  804.6 1.5 collective-permute-done.5
  813.8 1.3 collective-permute-start.8
  815.9 4.8 collective-permute-start.7
  820.8 1.4 collective-permute-done.7
  823.3 5.7 psum.7
  (457 shorter events, 85.2 us)
Async XLA Ops:
  0.0 19.0 %copy-start = (s32[16,26]{1,0:T(8,128)S(1)}, s32[16,26]{1,0:T(8,128)}, u32[]{:S(2)}) copy-start(s32[16,26]{1,0:T(8,128)} %param.26) | copy-start | bytes 4996
  1.2 40.7 %collective-permute-start.3 = (bf16[16,1,4,4,128]{4,0,3,2,1:T(8,128)(2,1)S(1)}, bf16[16,1,4,4,128]{4,0,3,2,1:T(8,128)(2,1)S(1)}, u32[]{:S(2)}, u32[]{:S(2)}) collective-permute-start(bf16[16,1,4,4,128]{4,0,3,2,1:T(8,128)(2,1)S(1)} %get-tuple-element.201), channel_id=1, source_target_pairs={{4,0},{8,4},{12,8},{16,12},{20,16},{24,20},{28,24},{5,1},{9,5},{13... | collective-permute-start | bytes 196616 | tf_op jit(solution)/shard_map/ppermute | solution.py:21
  2.5 39.4 %collective-permute-start.2 = (bf16[16,1,4,4,128]{4,0,3,2,1:T(8,128)(2,1)S(1)}, bf16[16,1,4,4,128]{4,0,3,2,1:T(8,128)(2,1)S(1)}, u32[]{:S(2)}, u32[]{:S(2)}) collective-permute-start(bf16[16,1,4,4,128]{4,0,3,2,1:T(8,128)(2,1)S(1)} %get-tuple-element.202), channel_id=1, source_target_pairs={{0,4},{4,8},{8,12},{12,16},{16,20},{20,24},{24,28},{1,5},{5,9},{9,... | collective-permute-start | bytes 196616 | tf_op jit(solution)/shard_map/ppermute | solution.py:21
  9.3 31.7 %collective-permute-start.1 = (bf16[2]{0:T(256)(128)(2,1)S(1)}, bf16[2]{0:T(256)(128)(2,1)S(1)}, u32[]{:S(2)}, u32[]{:S(2)}) collective-permute-start(bf16[2]{0:T(256)(128)(2,1)S(1)} %select_convert_fusion), channel_id=1, source_target_pairs={{4,0},{8,4},{12,8},{16,12},{20,16},{24,20},{28,24},{5,1},{9,5},{13... | collective-permute-start | bytes 20 | tf_op jit(solution)/shard_map/ppermute | solution.py:21
  10.6 30.4 %collective-permute-start = (bf16[2]{0:T(256)(128)(2,1)S(1)}, bf16[2]{0:T(256)(128)(2,1)S(1)}, u32[]{:S(2)}, u32[]{:S(2)}) collective-permute-start(bf16[2]{0:T(256)(128)(2,1)S(1)} %select_convert_fusion.1), channel_id=1, source_target_pairs={{0,4},{4,8},{8,12},{12,16},{16,20},{20,24},{24,28},{1,5},{5,9},{9,... | collective-permute-start | bytes 20 | tf_op jit(solution)/shard_map/ppermute | solution.py:21
  19.0 7.2 copy-start.36
  19.0 10.0 %copy-start.34 = (pred[16]{0:T(512)(128)(4,1)}, pred[16]{0:T(512)(128)(4,1)S(1)}, u32[]{:S(2)}) copy-start(pred[16]{0:T(512)(128)(4,1)S(1)} %get-tuple-element.254) | copy-start | bytes 52
  20.8 21.1 %copy-start.43 = (bf16[33]{0:T(256)(128)(2,1)}, bf16[33]{0:T(256)(128)(2,1)S(1)}, u32[]{:S(2)}) copy-start(bf16[33]{0:T(256)(128)(2,1)S(1)} %pad.92.clone) | copy-start | bytes 202
  22.4 6.6 copy-start.23
  22.5 6.7 copy-start.24
  22.6 6.6 copy-start.25
  22.6 6.6 copy-start.32
  22.7 28.0 %copy-start.38 = (pred[16]{0:T(512)(128)(4,1)}, pred[16]{0:T(512)(128)(4,1)S(1)}, u32[]{:S(2)}) copy-start(pred[16]{0:T(512)(128)(4,1)S(1)} %get-tuple-element.111) | copy-start | bytes 52
  22.7 25.3 %copy-start.30 = (pred[16]{0:T(512)(128)(4,1)}, pred[16]{0:T(512)(128)(4,1)S(1)}, u32[]{:S(2)}) copy-start(pred[16]{0:T(512)(128)(4,1)S(1)} %get-tuple-element.119) | copy-start | bytes 52
  22.7 25.9 %copy-start.26 = (pred[16]{0:T(512)(128)(4,1)}, pred[16]{0:T(512)(128)(4,1)S(1)}, u32[]{:S(2)}) copy-start(pred[16]{0:T(512)(128)(4,1)S(1)} %get-tuple-element.279) | copy-start | bytes 52
  22.8 24.6 %copy-start.21 = (s32[1024]{0:T(1024)}, s32[1024]{0:T(1024)S(1)}, u32[]{:S(2)}) copy-start(s32[1024]{0:T(1024)S(1)} %pad_clamp_fusion.25) | copy-start | bytes 12292
  22.8 25.3 %copy-start.19 = (s32[1024]{0:T(1024)}, s32[1024]{0:T(1024)S(1)}, u32[]{:S(2)}) copy-start(s32[1024]{0:T(1024)S(1)} %pad_clamp_fusion.26) | copy-start | bytes 12292
  22.8 27.2 %copy-start.28 = (pred[16]{0:T(512)(128)(4,1)}, pred[16]{0:T(512)(128)(4,1)S(1)}, u32[]{:S(2)}) copy-start(pred[16]{0:T(512)(128)(4,1)S(1)} %get-tuple-element.281) | copy-start | bytes 52
  22.9 26.6 %copy-start.22 = (s32[1024]{0:T(1024)}, s32[1024]{0:T(1024)S(1)}, u32[]{:S(2)}) copy-start(s32[1024]{0:T(1024)S(1)} %pad_clamp_fusion.28) | copy-start | bytes 12292
  22.9 27.2 %copy-start.20 = (s32[1024]{0:T(1024)}, s32[1024]{0:T(1024)S(1)}, u32[]{:S(2)}) copy-start(s32[1024]{0:T(1024)S(1)} %pad_clamp_fusion.29) | copy-start | bytes 12292
  23.6 27.2 %copy-start.11 = (bf16[16,4,1,1,128]{4,0,3,2,1:T(8,128)(2,1)}, bf16[16,4,1,1,128]{4,0,3,2,1:T(8,128)(2,1)S(1)}, u32[]{:S(2)}) copy-start(bf16[16,4,1,1,128]{4,0,3,2,1:T(8,128)(2,1)S(1)} %bitcast_select_fusion.16) | copy-start | bytes 49156
  24.9 25.8 %copy-start.12 = (bf16[16,4,1,1,128]{4,0,3,2,1:T(8,128)(2,1)}, bf16[16,4,1,1,128]{4,0,3,2,1:T(8,128)(2,1)S(1)}, u32[]{:S(2)}) copy-start(bf16[16,4,1,1,128]{4,0,3,2,1:T(8,128)(2,1)S(1)} %bitcast_select_fusion.17) | copy-start | bytes 49156
  27.5 23.2 %copy-start.13 = (bf16[16,4,1,1,128]{4,0,3,2,1:T(8,128)(2,1)}, bf16[16,4,1,1,128]{4,0,3,2,1:T(8,128)(2,1)S(1)}, u32[]{:S(2)}) copy-start(bf16[16,4,1,1,128]{4,0,3,2,1:T(8,128)(2,1)S(1)} %bitcast_select_fusion.18) | copy-start | bytes 49156
  28.9 21.9 %copy-start.14 = (bf16[16,4,1,1,128]{4,0,3,2,1:T(8,128)(2,1)}, bf16[16,4,1,1,128]{4,0,3,2,1:T(8,128)(2,1)S(1)}, u32[]{:S(2)}) copy-start(bf16[16,4,1,1,128]{4,0,3,2,1:T(8,128)(2,1)S(1)} %bitcast_select_fusion.19) | copy-start | bytes 49156
  41.3 9.5 %copy-start.50 = (s32[8]{0:T(128)}, s32[8]{0:T(128)S(1)}, u32[]{:S(2)}) copy-start(s32[8]{0:T(128)S(1)} %select_reduce_fusion.1) | copy-start | bytes 100
  52.3 5.8 copy-start.9
  53.1 5.0 copy-start.17
  53.1 5.7 copy-start.16
  110.2 4.2 copy-start.33
  110.2 5.1 copy-start.35
  116.2 654.0 %collective-permute-start.4 = (bf16[16,1,4,4,128]{4,0,3,2,1:T(8,128)(2,1)}, bf16[16,1,4,4,128]{4,0,3,2,1:T(8,128)(2,1)}, u32[]{:S(2)}, u32[]{:S(2)}) collective-permute-start(bf16[16,1,4,4,128]{4,0,3,2,1:T(8,128)(2,1)} %slice.1336), channel_id=1, source_target_pairs={{0,4},{4,8},{8,12},{12,16},{16,20},{20,24},{24,28},{1,5},{5,9},{9,... | collective-permute-start | bytes 196616 | tf_op jit(solution)/shard_map/ppermute | solution.py:21
  757.7 12.1 %copy-start.18 = (bf16[16,2,2,2,128]{4,0,3,2,1:T(8,128)(2,1)S(1)}, bf16[16,2,2,2,128]{4,0,3,2,1:T(8,128)(2,1)}, u32[]{:S(2)}) copy-start(bf16[16,2,2,2,128]{4,0,3,2,1:T(8,128)(2,1)} %get-tuple-element.197) | copy-start | bytes 98308
  757.8 12.5 %copy-start.44 = (bf16[33]{0:T(256)(128)(2,1)S(1)}, bf16[33]{0:T(256)(128)(2,1)}, u32[]{:S(2)}) copy-start(bf16[33]{0:T(256)(128)(2,1)} %copy-done.43) | copy-start | bytes 202
  757.8 14.4 %copy-start.31 = (pred[16]{0:T(512)(128)(4,1)S(1)}, pred[16]{0:T(512)(128)(4,1)}, u32[]{:S(2)}) copy-start(pred[16]{0:T(512)(128)(4,1)} %copy-done.30) | copy-start | bytes 52
  759.4 13.7 %copy-start.27 = (pred[16]{0:T(512)(128)(4,1)S(1)}, pred[16]{0:T(512)(128)(4,1)}, u32[]{:S(2)}) copy-start(pred[16]{0:T(512)(128)(4,1)} %copy-done.26) | copy-start | bytes 52
  760.9 13.0 %copy-start.29 = (pred[16]{0:T(512)(128)(4,1)S(1)}, pred[16]{0:T(512)(128)(4,1)}, u32[]{:S(2)}) copy-start(pred[16]{0:T(512)(128)(4,1)} %copy-done.28) | copy-start | bytes 52
  762.1 12.6 %copy-start.39 = (pred[16]{0:T(512)(128)(4,1)S(1)}, pred[16]{0:T(512)(128)(4,1)}, u32[]{:S(2)}) copy-start(pred[16]{0:T(512)(128)(4,1)} %copy-done.38) | copy-start | bytes 52
  775.1 5.4 copy-start.40
  781.4 23.1 %copy-start.49 = (pred[8]{0:T(512)(128)(4,1)S(1)}, pred[8]{0:T(512)(128)(4,1)}, u32[]{:S(2)}) copy-start(pred[8]{0:T(512)(128)(4,1)} %copy-done.48) | copy-start | bytes 28
  781.4 23.1 %copy-start.51 = (s32[8]{0:T(128)S(1)}, s32[8]{0:T(128)}, u32[]{:S(2)}) copy-start(s32[8]{0:T(128)} %copy-done.50) | copy-start | bytes 100
  798.7 5.9 collective-permute-start.6
  800.0 6.1 collective-permute-start.5
  810.4 5.4 copy-start.41
  810.6 10.2 %copy-start.47 = (s32[8]{0:T(128)S(1)}, s32[8]{0:T(128)}, u32[]{:S(2)}) copy-start(s32[8]{0:T(128)} %fusion.176) | copy-start | bytes 100
  810.6 11.6 %copy-start.46 = (bf16[9]{0:T(256)(128)(2,1)S(1)}, bf16[9]{0:T(256)(128)(2,1)}, u32[]{:S(2)}) copy-start(bf16[9]{0:T(256)(128)(2,1)} %pad.12.clone) | copy-start | bytes 58
  811.1 17.8 %copy-start.45 = (f32[64]{0:T(128)S(1)}, f32[64]{0:T(128)}, u32[]{:S(2)}) copy-start(f32[64]{0:T(128)} %param.33) | copy-start | bytes 772
  813.8 7.0 collective-permute-start.8
  815.9 6.3 collective-permute-start.7
  (13 other events, 25.8 us)
where the time goes:
time: 834 us; the launch traced here: 830 us
  local copies, waits for them, and re-layouts  709 us (85%)
  blocking collectives  37.1 us (4%)
  other arithmetic  33.5 us (4%)
  starting transfers between devices  31 us (4%)
  matrix products  14.3 us (2%)
    slice x70, local copies, waits for them, and re-layouts, apply_taps(): padded[:, stride_span(1 + a, counts[0], stride), stride_span(1 + b, count...  657 us
    gather x33, local copies, waits for them, and re-layouts, surround(): fragment = jnp.take(trimmed, row_index, axis=0)  29.7 us
    ppermute x7, starting transfers between devices, passed_along(): lax.ppermute(value, axis, [(source, source + steps) for source in range(f...  25.1 us
  transfers between devices with their start and end apart: 9, of which 2 were waited for; matrix products, arithmetic and copies ran while one was open for 81% of the time, Pallas kernels for 0%

commit v1 on v0

v1 whole, which is shorter than its diff:
```python
import functools

import jax
import jax.numpy as jnp
from jax import lax
from jax.experimental import pallas as pl
from jax.experimental.pallas import tpu as pltpu
from jax.sharding import PartitionSpec as P

EDGE = 4
SLAB_Y = 4
SLAB_Z = 4
NY = SLAB_Y * EDGE
NZ = SLAB_Z * EDGE
LAYER = NY * NZ
NX = 2 * EDGE
CY = NY // 2
CZ = NZ // 2
CLAYER = CY * CZ
CX = NX // 2
FACE = EDGE * EDGE
epsilon = 1e-06
BF = jnp.bfloat16
F32 = jnp.float32
NT = (((1,), (1,)), ((), ()))


def iota(shape, dim):
    return lax.broadcasted_iota(jnp.int32, shape, dim)


def one(cond):
    return jnp.where(cond, 1.0, 0.0).astype(BF)


def pick(a, b):
    return jnp.dot(a, b, preferred_element_type=F32)


def fused_kernel(
    n_space,
    n_chan,
    bricks,
    slots,
    feat,
    meta,
    wf,
    wd_hbm,
    wc_hbm,
    gain,
    out,
    wd,
    wc,
    fh,
    mh,
    s_buf,
    mask,
    g_buf,
    perm_h,
    perm_c,
    sel_d,
    sel_c,
    d_buf,
    c_buf,
    e_buf,
    pb,
    pw,
    ohd,
    wsem,
    s1,
    r1,
    s2,
    r2,
    hs2,
    hr2,
    s3,
    r3,
    hs3,
    hr3,
    s4,
    r4,
    ws4,
    wr4,
):
    sp = lax.axis_index("space")
    me = lax.axis_index("chan")
    has_prev = sp > 0
    has_next = sp < n_space - 1
    fine = feat.shape[2]
    wide = fine // n_chan
    parents = (SLAB_Y // 2) * (SLAB_Z // 2)
    cells = EDGE**3
    coarse_own = wd.shape[0]
    coarse = coarse_own * n_chan
    taps2 = 9

    def rc(src, dst, ss, rs, space, chan):
        return pltpu.make_async_remote_copy(
            src_ref=src,
            dst_ref=dst,
            send_sem=ss,
            recv_sem=rs,
            device_id={"space": space, "chan": chan},
            device_id_type=pl.DeviceIdType.MESH,
        )

    copy_d = pltpu.make_async_copy(wd_hbm, wd, wsem.at[0])
    copy_c = pltpu.make_async_copy(wc_hbm, wc, wsem.at[1])
    copy_d.start()
    copy_c.start()
    peers = [lax.rem(me + k, n_chan) for k in range(1, n_chan)]

    barrier = pltpu.get_barrier_semaphore()

    def greet(space, chan):
        pl.semaphore_signal(
            barrier,
            inc=1,
            device_id={"space": space, "chan": chan},
            device_id_type=pl.DeviceIdType.MESH,
        )

    for chan in peers:
        greet(sp, chan)

    @pl.when(has_prev)
    def _():
        for chan in range(n_chan):
            greet(sp - 1, chan)

    @pl.when(has_next)
    def _():
        for chan in range(n_chan):
            greet(sp + 1, chan)

    pl.semaphore_wait(
        barrier, n_chan - 1 + n_chan * (has_prev.astype(jnp.int32) + has_next.astype(jnp.int32))
    )

    up_feat = rc(feat.at[:, pl.ds((EDGE - 1) * FACE, FACE), :], fh.at[0], s1.at[0, 0], r1.at[0, 0], sp + 1, me)
    up_meta = rc(meta, mh.at[0], s1.at[0, 1], r1.at[0, 1], sp + 1, me)
    dn_feat = rc(feat.at[:, pl.ds(0, FACE), :], fh.at[1], s1.at[1, 0], r1.at[1, 0], sp - 1, me)
    dn_meta = rc(meta, mh.at[1], s1.at[1, 1], r1.at[1, 1], sp - 1, me)

    @pl.when(has_next)
    def _():
        up_meta.start()
        up_feat.start()

    @pl.when(has_prev)
    def _():
        dn_meta.start()
        dn_feat.start()

    @pl.when(jnp.logical_not(has_prev))
    def _():
        fh[0] = jnp.zeros(fh.shape[1:], BF)
        mh[0] = jnp.zeros(mh.shape[1:], jnp.int32)
        g_buf[0] = jnp.zeros(g_buf.shape[1:], BF)
        c_buf[0] = jnp.zeros(c_buf.shape[1:], BF)
        pb[0] = jnp.zeros(pb.shape[1:], BF)
        pw[0] = jnp.zeros(pw.shape[1:], F32)

    @pl.when(jnp.logical_not(has_next))
    def _():
        fh[1] = jnp.zeros(fh.shape[1:], BF)
        mh[1] = jnp.zeros(mh.shape[1:], jnp.int32)
        c_buf[CX + 1] = jnp.zeros(c_buf.shape[1:], BF)
        pb[2] = jnp.zeros(pb.shape[1:], BF)
        pw[2] = jnp.zeros(pw.shape[1:], F32)

    lanes = meta.shape[1]
    columns = bricks * FACE
    spread = jnp.where(iota((lanes, columns), 1) // FACE == iota((lanes, columns), 0), 1.0, 0.0)
    face = iota((1, columns), 1) % FACE
    row_ids = iota((LAYER, columns), 0)

    def keys_of(meta_block):
        code = jnp.dot(meta_block.astype(F32), spread, preferred_element_type=F32)[0:1].astype(jnp.int32)
        x_bit = code % 2
        y_pos = code // 2 % SLAB_Y
        z_pos = code // (2 * SLAB_Y)
        y = y_pos * EDGE + face // EDGE
        z = z_pos * EDGE + face % EDGE
        return x_bit, y, z

    def one_hot(key, x_want, c):
        x_bit, y, z = key
        fits = (x_bit == x_want) & (z - c >= 0) & (z - c < NZ)
        return one(row_ids == jnp.where(fits, y * NZ + z - c, -1))

    blank_y = jnp.zeros((NX + 2, NZ, 3 * fine), BF)
    s_buf[:, 0:NZ, :] = blank_y
    s_buf[:, NZ + LAYER : 2 * NZ + LAYER, :] = blank_y

    faces = jnp.concatenate(
        [feat[:, i * FACE : (i + 1) * FACE, :].reshape(columns, fine) for i in range(EDGE)], axis=1
    )
    key = keys_of(meta[...])
    for x in range(2):
        for c in (-1, 0, 1):
            hot = one_hot(key, x, c)
            placed = pick(hot, faces).astype(BF)
            for i in range(EDGE):
                s_buf[1 + EDGE * x + i, NZ : NZ + LAYER, (c + 1) * fine : (c + 2) * fine] = placed[
                    :, i * fine : (i + 1) * fine
                ]
            if c == 0:
                mask[x] = pick(hot, jnp.ones((columns, fine), BF))

    def hidden_layer(x):
        parts = []
        for a in (-1, 0, 1):
            for b in (-1, 0, 1):
                parts.append(s_buf[x + 1 + a, (1 + b) * NZ : (1 + b) * NZ + LAYER, :])
        total = lax.dot_general(jnp.concatenate(parts, axis=1), wf[...], NT, preferred_element_type=F32)
        total = jnp.where(mask[x // EDGE][:, 0:wide] > 0.5, jnp.maximum(total, 0.0), 0.0)
        rows = LAYER // n_chan
        packed = jnp.concatenate([total[j * rows : (j + 1) * rows] for j in range(n_chan)], axis=1)
        g_buf[x + 1, me] = packed.astype(BF)
        for k, chan in enumerate(peers):
            rc(g_buf.at[x + 1, me], g_buf.at[x + 1, me], s2.at[x, k], r2.at[x, me], sp, chan).start()

    for x in range(1, NX - 1):
        hidden_layer(x)

    def halo_layer(side):
        k = keys_of(mh[side])
        block = fh[side].reshape(columns, fine)
        for c in (-1, 0, 1):
            s_buf[0 if side == 0 else NX + 1, NZ : NZ + LAYER, (c + 1) * fine : (c + 2) * fine] = pick(
                one_hot(k, 1 - side, c), block
            ).astype(BF)

    @pl.when(has_next)
    def _():
        dn_meta.wait_recv()
        dn_feat.wait_recv()

    halo_layer(1)
    hidden_layer(NX - 1)

    @pl.when(has_next)
    def _():
        for chan in range(n_chan):
            rc(g_buf.at[NX, me], g_buf.at[0, me], hs2.at[chan], hr2.at[me], sp + 1, chan).start()

    @pl.when(has_prev)
    def _():
        up_meta.wait_recv()
        up_feat.wait_recv()

    halo_layer(0)
    hidden_layer(0)

    big = n_chan * fine
    r, q = iota((big, big), 0), iota((big, big), 1)
    perm_h[...] = one((r % fine) // wide * fine + r // fine * wide + r % wide == q)
    half = fine // coarse_own
    big2 = n_chan * fine
    perm_c[...] = one((r % fine) // coarse_own * coarse + r // fine * coarse_own + r % coarse_own == q)
    del big2

    r, q = iota((taps2 * CLAYER, LAYER), 0), iota((taps2 * CLAYER, LAYER), 1)
    bc, at = r // CLAYER, r % CLAYER
    y = 2 * (at // CZ) + bc // 3 - 1
    z = 2 * (at % CZ) + bc % 3 - 1
    sel_d[...] = one((y >= 0) & (z >= 0) & (y * NZ + z == q))
    r, q = iota((taps2 * CLAYER, CLAYER), 0), iota((taps2 * CLAYER, CLAYER), 1)
    bc, at = r // CLAYER, r % CLAYER
    par, yz = at // FACE, at % FACE
    y = par // (SLAB_Z // 2) * EDGE + yz // EDGE + bc // 3 - 1
    z = par % (SLAB_Z // 2) * EDGE + yz % EDGE + bc % 3 - 1
    sel_c[...] = one((y >= 0) & (z >= 0) & (z < CZ) & (y * CZ + z == q))

    lane_par = jnp.where(
        iota((lanes, parents * cells), 1) // cells == iota((lanes, parents * cells), 0), 1.0, 0.0
    )
    out_ids = iota((slots * cells, parents * cells), 0)
    for k in range(3):
        block = meta[...] if k == 1 else mh[k // 2]
        rel = jnp.dot(block.astype(F32), lane_par, preferred_element_type=F32)[1:2].astype(jnp.int32)
        slot = rel - (2 - k) * slots
        target = slot * cells + iota((1, parents * cells), 1) % cells
        ohd[k] = one(out_ids == jnp.where((slot >= 0) & (slot < slots), target, -1))

    for x in range(NX):
        for k in range(1, n_chan):
            src = lax.rem(me + k, n_chan)
            rc(g_buf.at[x + 1, src], g_buf.at[x + 1, src], s2.at[x, 0], r2.at[x, src], sp, src).wait_recv()

    @pl.when(has_prev)
    def _():
        for chan in range(n_chan):
            rc(g_buf.at[0, chan], g_buf.at[0, chan], hs2.at[chan], hr2.at[chan], sp - 1, chan).wait_recv()

    gathered = jnp.concatenate(
        [jnp.concatenate([g_buf[x, s] for s in range(n_chan)], axis=1) for x in range(NX + 1)], axis=0
    )
    rows = LAYER // n_chan
    spread_h = pick(gathered, perm_h[...]).astype(BF)
    layers = [
        jnp.concatenate(
            [spread_h[x * rows : (x + 1) * rows, j * fine : (j + 1) * fine] for j in range(n_chan)], axis=0
        )
        for x in range(NX + 1)
    ]
    d_buf[...] = pick(sel_d[...], jnp.concatenate(layers, axis=1)).astype(BF)

    copy_d.wait()
    stacked = []
    for x in range(CX):
        stacked.append(
            jnp.concatenate(
                [
                    d_buf[bc * CLAYER : (bc + 1) * CLAYER, (2 * x + a) * fine : (2 * x + a + 1) * fine]
                    for a in range(3)
                    for bc in range(taps2)
                ],
                axis=1,
            )
        )
    pieces = lax.dot_general(jnp.concatenate(stacked, axis=0), wd[...], NT, preferred_element_type=F32)
    crows = CLAYER // half
    for x in range(CX):
        live = pick(sel_d[4 * CLAYER : 5 * CLAYER, :], mask[x // 2].astype(BF))[:, 0:coarse_own]
        part = pieces[x * CLAYER : (x + 1) * CLAYER]
        part = jnp.where(live > 0.5, jnp.maximum(part, 0.0), 0.0)
        c_buf[x + 1, me] = jnp.concatenate(
            [part[j * crows : (j + 1) * crows] for j in range(half)], axis=1
        ).astype(BF)

    @pl.when(has_next)
    def _():
        for chan in range(n_chan):
            rc(c_buf.at[CX, me], c_buf.at[0, me], hs3.at[0, chan], hr3.at[0, me], sp + 1, chan).start()

    @pl.when(has_prev)
    def _():
        for chan in range(n_chan):
            rc(c_buf.at[1, me], c_buf.at[CX + 1, me], hs3.at[1, chan], hr3.at[1, me], sp - 1, chan).start()

    own_c = c_buf.at[pl.ds(1, CX), me]
    for k, chan in enumerate(peers):
        rc(own_c, own_c, s3.at[k], r3.at[me], sp, chan).start()
    for k in range(1, n_chan):
        src = lax.rem(me + k, n_chan)
        ref = c_buf.at[pl.ds(1, CX), src]
        rc(ref, ref, s3.at[0], r3.at[src], sp, src).wait_recv()

    @pl.when(has_prev)
    def _():
        for chan in range(n_chan):
            ref = c_buf.at[0, chan]
            rc(ref, ref, hs3.at[0, chan], hr3.at[0, chan], sp - 1, chan).wait_recv()

    @pl.when(has_next)
    def _():
        for chan in range(n_chan):
            ref = c_buf.at[CX + 1, chan]
            rc(ref, ref, hs3.at[1, chan], hr3.at[1, chan], sp + 1, chan).wait_recv()

    gathered = jnp.concatenate(
        [jnp.concatenate([c_buf[x, s] for s in range(n_chan)], axis=1) for x in range(CX + 2)], axis=0
    )
    spread_c = pick(gathered, perm_c[...]).astype(BF)
    layers = [
        jnp.concatenate(
            [spread_c[x * crows : (x + 1) * crows, j * coarse : (j + 1) * coarse] for j in range(half)], axis=0
        )
        for x in range(CX + 2)
    ]
    e_buf[...] = pick(sel_c[...], jnp.concatenate(layers, axis=1)).astype(BF)
    copy_c.wait()
    total = None
    for a in range(3):
        for bc in range(taps2):
            block = jnp.concatenate(
                [
                    e_buf[
                        bc * CLAYER + g * FACE : bc * CLAYER + (g + 1) * FACE,
                        (x + a) * coarse : (x + a + 1) * coarse,
                    ]
                    for g in range(parents)
                    for x in range(CX)
                ],
                axis=0,
            )
            t = a * taps2 + bc
            term = lax.dot_general(wc[:, t * coarse : (t + 1) * coarse], block, NT, preferred_element_type=F32)
            total = term if total is None else total + term
    rounded = total.astype(BF)
    pb[1] = rounded
    values = rounded.astype(F32)
    pw[1, me] = jnp.sum(values * values, axis=0, keepdims=True)

    for k, chan in enumerate(peers):
        rc(pw.at[1, me], pw.at[1, me], ws4.at[1, k], wr4.at[1, me], sp, chan).start()

    @pl.when(has_next)
    def _():
        rc(pb.at[1], pb.at[0], s4.at[0], r4.at[0], sp + 1, me).start()
        for chan in range(n_chan):
            rc(pw.at[1, me], pw.at[0, me], ws4.at[0, chan], wr4.at[0, me], sp + 1, chan).start()

    @pl.when(has_prev)
    def _():
        rc(pb.at[1], pb.at[2], s4.at[1], r4.at[1], sp - 1, me).start()
        for chan in range(n_chan):
            rc(pw.at[1, me], pw.at[2, me], ws4.at[2, chan], wr4.at[2, me], sp - 1, chan).start()

    own = gain.shape[1]
    gain_col = jnp.sum(
        jnp.where(iota((own, own), 0) == iota((own, own), 1), gain[...], 0.0), axis=1, keepdims=True
    )

    def normed(k):
        power = pw[k, 0]
        for s in range(1, n_chan):
            power = power + pw[k, s]
        scaled = pb[k].astype(F32) * lax.rsqrt(power / coarse + epsilon) * gain_col
        return lax.dot_general(scaled.astype(BF), ohd[k], NT, preferred_element_type=F32)

    for k in range(1, n_chan):
        src = lax.rem(me + k, n_chan)
        rc(pw.at[1, src], pw.at[1, src], ws4.at[1, 0], wr4.at[1, src], sp, src).wait_recv()
    result = normed(1)

    @pl.when(has_prev)
    def _():
        rc(pb.at[0], pb.at[0], s4.at[0], r4.at[0], sp - 1, me).wait_recv()
        for chan in range(n_chan):
            rc(pw.at[0, chan], pw.at[0, chan], ws4.at[0, chan], wr4.at[0, chan], sp - 1, chan).wait_recv()

    @pl.when(has_next)
    def _():
        rc(pb.at[2], pb.at[2], s4.at[1], r4.at[1], sp + 1, me).wait_recv()
        for chan in range(n_chan):
            rc(pw.at[2, chan], pw.at[2, chan], ws4.at[2, chan], wr4.at[2, chan], sp + 1, chan).wait_recv()

    out[...] = (result + normed(0) + normed(2)).astype(BF)

    for x in range(NX):
        for k, chan in enumerate(peers):
            rc(g_buf.at[x + 1, me], g_buf.at[x + 1, me], s2.at[x, k], r2.at[x, me], sp, chan).wait_send()
    for k, chan in enumerate(peers):
        rc(own_c, own_c, s3.at[k], r3.at[me], sp, chan).wait_send()
        rc(pw.at[1, me], pw.at[1, me], ws4.at[1, k], wr4.at[1, me], sp, chan).wait_send()

    @pl.when(has_next)
    def _():
        up_meta.wait_send()
        up_feat.wait_send()
        rc(pb.at[1], pb.at[0], s4.at[0], r4.at[0], sp + 1, me).wait_send()
        for chan in range(n_chan):
            rc(g_buf.at[NX, me], g_buf.at[0, me], hs2.at[chan], hr2.at[me], sp + 1, chan).wait_send()
            rc(c_buf.at[CX, me], c_buf.at[0, me], hs3.at[0, chan], hr3.at[0, me], sp + 1, chan).wait_send()
            rc(pw.at[1, me], pw.at[0, me], ws4.at[0, chan], wr4.at[0, me], sp + 1, chan).wait_send()

    @pl.when(has_prev)
    def _():
        dn_meta.wait_send()
        dn_feat.wait_send()
        rc(pb.at[1], pb.at[2], s4.at[1], r4.at[1], sp - 1, me).wait_send()
        for chan in range(n_chan):
            rc(c_buf.at[1, me], c_buf.at[CX + 1, me], hs3.at[1, chan], hr3.at[1, me], sp - 1, chan).wait_send()
            rc(pw.at[1, me], pw.at[2, me], ws4.at[2, chan], wr4.at[2, me], sp - 1, chan).wait_send()


def body(n_space, n_chan, features, neighbours, parent_index, octant, parent_dest, conv_fine, conv_down, conv_coarse, norm_gain):
    device = lax.axis_index("space")
    bricks, _, fine = features.shape
    parents = parent_dest.shape[0]
    slots = 2 * parents
    local = parent_index - device * parents
    y_pos = 2 * (local // (SLAB_Z // 2)) + octant // 2 % 2
    z_pos = 2 * (local % (SLAB_Z // 2)) + octant // 4
    code = octant % 2 + 2 * y_pos + 2 * SLAB_Y * z_pos
    rel = parent_dest - (device - 1) * slots
    meta = jnp.concatenate(
        [jnp.pad(code, (0, 128 - bricks))[None], jnp.pad(rel, (0, 128 - parents))[None], jnp.zeros((6, 128), jnp.int32)], 0
    )
    down = conv_down.shape[0]
    own = conv_coarse.shape[0]
    cells = EDGE**3
    coarse = down * n_chan
    vmem = pl.BlockSpec(memory_space=pltpu.VMEM)
    hbm = pl.BlockSpec(memory_space=pl.ANY)
    dma = pltpu.SemaphoreType.DMA
    big = n_chan * fine
    crows = CLAYER // (fine // down)
    return pl.pallas_call(
        functools.partial(fused_kernel, n_space, n_chan, bricks, slots),
        out_shape=jax.ShapeDtypeStruct((own, slots * cells), BF),
        in_specs=[vmem, vmem, vmem, hbm, hbm, vmem],
        out_specs=vmem,
        scratch_shapes=[
            pltpu.VMEM(conv_down.shape, BF),
            pltpu.VMEM(conv_coarse.shape, BF),
            pltpu.VMEM((2, bricks, FACE, fine), BF),
            pltpu.VMEM((2, 8, 128), jnp.int32),
            pltpu.VMEM((NX + 2, LAYER + 2 * NZ, 3 * fine), BF),
            pltpu.VMEM((2, LAYER, fine), F32),
            pltpu.VMEM((NX + 1, n_chan, LAYER // n_chan, fine), BF),
            pltpu.VMEM((big, big), BF),
            pltpu.VMEM((big, big), BF),
            pltpu.VMEM((9 * CLAYER, LAYER), BF),
            pltpu.VMEM((9 * CLAYER, CLAYER), BF),
            pltpu.VMEM((9 * CLAYER, (NX + 1) * fine), BF),
            pltpu.VMEM((CX + 2, n_chan, crows, fine), BF),
            pltpu.VMEM((9 * CLAYER, (CX + 2) * coarse), BF),
            pltpu.VMEM((3, own, parents * cells), BF),
            pltpu.VMEM((3, n_chan, 1, parents * cells), F32),
            pltpu.VMEM((3, slots * cells, parents * cells), BF),
            dma((2,)),
            dma((2, 2)),
            dma((2, 2)),
            dma((NX, n_chan - 1)),
            dma((NX, n_chan)),
            dma((n_chan,)),
            dma((n_chan,)),
            dma((n_chan - 1,)),
            dma((n_chan,)),
            dma((2, n_chan)),
            dma((2, n_chan)),
            dma((2,)),
            dma((2,)),
            dma((3, n_chan)),
            dma((3, n_chan)),
        ],
        compiler_params=pltpu.CompilerParams(collective_id=0, has_side_effects=True),
    )(features, meta, conv_fine, conv_down, conv_coarse, norm_gain.reshape(1, -1))


def solution(mesh):
    sizes = dict(mesh.shape)
    return jax.shard_map(
        functools.partial(body, sizes["space"], sizes["chan"]),
        mesh=mesh,
        in_specs=(
            P("space", None, None),
            P("space", None),
            P("space"),
            P("space"),
            P("space"),
            P("chan", None),
            P("chan", None),
            P("chan", None),
            P("chan"),
        ),
        out_specs=P("chan", "space"),
        check_vma=False,
    )
```

time: 834 us -> 36.5 us (0.04)
  local copies, waits for them, and re-layouts: 709 us -> 2.88 us
  blocking collectives: 37.1 us -> 0 us
  other arithmetic: 33.5 us -> 0.69 us
  Pallas kernels: 0 us -> 32.7 us
  starting transfers between devices: 31 us -> 0 us
  matrix products: 14.3 us -> 0 us
    slice x74 -> x0, local copies, waits for them, and re-layouts: 658 us -> none  [the longest x70 657 us: apply_taps(): padded[:, stride_span(1 + a, counts[0], stride), stride_span(1 + b, count...]
    pallas_call x0 -> x1, Pallas kernels: none -> 32.7 us  [body(): pl.pallas_call(functools.partial(fused_kernel, n_space, n_chan, bricks, s...]
    gather x38 -> x0, local copies, waits for them, and re-layouts: 32.7 us -> none  [the longest x33 29.7 us: surround(): fragment = jnp.take(trimmed, row_index, axis=0)]
    all_gather x2 -> x0, blocking collectives: 31.5 us -> none  [the longest x1 15.9 us: body(): widened = lax.all_gather(hidden, 'chan', axis=4, tiled=True)]
    ppermute x9 -> x0, starting transfers between devices: 31 us -> none  [the longest x7 25.1 us: passed_along(): lax.ppermute(value, axis, [(source, source + steps) for source in range(f...]
    dot_general x81 -> x0, matrix products: 14.3 us -> none  [apply_taps(): lax.dot_general(window.reshape(-1, in_width), tap_block, (((1,), (1,)), (...]
    select_n x44 -> x0, other arithmetic: 14 us -> none  [the longest x37 11.2 us: surround(): fragment = jnp.take(trimmed, row_index, axis=0)]
  transfers between devices with their start and end apart: 9 -> 0, of which waited for: 2 -> 0; matrix products, arithmetic and copies ran while one was open for 81% -> 0% of each run, Pallas kernels for 0% -> 0%
where the time goes in v1:
time: 36.5 us; the launch traced here: 36.3 us
  Pallas kernels  32.7 us (90%)
  local copies, waits for them, and re-layouts  2.88 us (8%)
  other arithmetic  0.69 us (2%)
    pallas_call x1, Pallas kernels, body(): pl.pallas_call(functools.partial(fused_kernel, n_space, n_chan, bricks, s...  32.7 us
    unnamed x7, local copies, waits for them, and re-layouts  2.79 us

profile of v1, /device:TPU:0, one launch (start us, length us, event | category | flops | bytes accessed | tf_op | source)
XLA Modules:
  0.0 36.3 jit_solution(6510628698823680393)
XLA Ops:
  0.0 0.0 copy-start.2
  0.0 0.7 %copy-done.2 = s32[4]{0:T(128)S(1)} copy-done((s32[4]{0:T(128)S(1)}, s32[4]{0:T(128)}, u32[]{:S(2)}) %copy-start.2) | copy-done | bytes 40
  0.7 0.0 copy-start
  0.7 0.0 copy-start.1
  0.7 0.6 %copy-done = s32[16]{0:T(128)S(1)} copy-done((s32[16]{0:T(128)S(1)}, s32[16]{0:T(128)}, u32[]{:S(2)}) %copy-start) | copy-done | bytes 88
  1.3 0.0 copy-done.1
  1.4 0.1 pad.12.clone
  1.4 0.7 %add_add_fusion.meta = s32[8,128]{1,0:T(8,128)} fusion(s32[1,128]{1,0:T(1,128)S(1)} %get-tuple-element.5, s32[1,128]{1,0:T(1,128)S(1)} %get-tuple-element.6, s32[8]{0:T(128)S(1)} %pad.12.clone), kind=kLoop, calls=%fused_computation | loop fusion | flops 2048 | bytes 5152 | tf_op jit(solution)/shard_map/concatenate | solution.py:480
  2.1 32.7 %shard_map.82 = bf16[64,512]{1,0:T(8,128)(2,1)} custom-call(bf16[16,64,128]{2,1,0:T(8,128)(2,1)} %feat.1, s32[8,128]{1,0:T(8,128)} %add_add_fusion.meta, bf16[32,3456]{1,0:T(8,128)(2,1)} %wf.1, bf16[64,3456]{1,0:T(8,128)(2,1)} %wd_hbm.1, bf16[64,6912]{1,0:T(8,128)(2,1)} %wc_hbm.1, f32[1,64]{1,0:T(1,128)} %bitcast.5), custom_call_target="tpu_custom_call" | custom-call | tf_op jit(solution)/shard_map/pallas_call | solution.py:492
  34.8 1.5 %copy.10 = bf16[64,512]{1,0:T(8,128)(2,1)} copy(bf16[64,512]{1,0:T(8,128)(2,1)} %shard_map.82) | data formatting | bytes 131072
  (4 shorter events, 0.0 us)
Async XLA Ops:
  0.0 0.7 %copy-start.2 = (s32[4]{0:T(128)S(1)}, s32[4]{0:T(128)}, u32[]{:S(2)}) copy-start(s32[4]{0:T(128)} %param.12) | copy-start | bytes 52
  0.7 0.7 %copy-start = (s32[16]{0:T(128)S(1)}, s32[16]{0:T(128)}, u32[]{:S(2)}) copy-start(s32[16]{0:T(128)} %param.10) | copy-start | bytes 196
  0.7 0.7 %copy-start.1 = (s32[16]{0:T(128)S(1)}, s32[16]{0:T(128)}, u32[]{:S(2)}) copy-start(s32[16]{0:T(128)} %param.11) | copy-start | bytes 196

commit v2 on v1

--- a/solution.py
+++ b/solution.py
@@ -2,6 +2,7 @@
 
 import jax
 import jax.numpy as jnp
+import numpy as np
 from jax import lax
 from jax.experimental import pallas as pl
 from jax.experimental.pallas import tpu as pltpu
@@ -37,50 +38,40 @@
     return jnp.dot(a, b, preferred_element_type=F32)
 
 
+def tables(n_chan, fine, coarse_own):
+    def held(cond):
+        return jnp.asarray(np.asarray(cond, np.float32).astype(jnp.bfloat16))
+
+    def grid(rows, columns):
+        return np.arange(rows)[:, None], np.arange(columns)[None, :]
+
+    wide = fine // n_chan
+    coarse = coarse_own * n_chan
+    r, q = grid(n_chan * fine, n_chan * fine)
+    perm_h = held((r % fine) // wide * fine + r // fine * wide + r % wide == q)
+    perm_c = held((r % fine) // coarse_own * coarse + r // fine * coarse_own + r % coarse_own == q)
+    r, q = grid(9 * CLAYER, LAYER)
+    bc, at = r // CLAYER, r % CLAYER
+    y = 2 * (at // CZ) + bc // 3 - 1
+    z = 2 * (at % CZ) + bc % 3 - 1
+    sel_d = held((y >= 0) & (z >= 0) & (y * NZ + z == q))
+    r, q = grid(9 * CLAYER, CLAYER)
+    bc, at = r // CLAYER, r % CLAYER
+    par, yz = at // FACE, at % FACE
+    y = par // (SLAB_Z // 2) * EDGE + yz // EDGE + bc // 3 - 1
+    z = par % (SLAB_Z // 2) * EDGE + yz % EDGE + bc % 3 - 1
+    sel_c = held((y >= 0) & (z >= 0) & (z < CZ) & (y * CZ + z == q))
+    return perm_h, perm_c, sel_d, sel_c
+
+
 def fused_kernel(
-    n_space,
-    n_chan,
-    bricks,
-    slots,
-    feat,
-    meta,
-    wf,
-    wd_hbm,
-    wc_hbm,
-    gain,
+    n_space, n_chan, bricks, slots,
+    feat_hbm, parent_hbm, octant_hbm, dest_hbm, wf_hbm, wd_hbm, wc_hbm, gain_hbm,
+    perm_h_hbm, perm_c_hbm, sel_d_hbm, sel_c_hbm,
     out,
-    wd,
-    wc,
-    fh,
-    mh,
-    s_buf,
-    mask,
-    g_buf,
-    perm_h,
-    perm_c,
-    sel_d,
-    sel_c,
-    d_buf,
-    c_buf,
-    e_buf,
-    pb,
-    pw,
-    ohd,
-    wsem,
-    s1,
-    r1,
-    s2,
-    r2,
-    hs2,
-    hr2,
-    s3,
-    r3,
-    hs3,
-    hr3,
-    s4,
-    r4,
-    ws4,
-    wr4,
+    feat, wf, gain, parent_in, octant_in, dest_in, meta, wd, wc, fh, mh, s_buf, mask, g_buf,
+    perm_h, perm_c, sel_d, sel_c, d_buf, c_buf, e_buf, pb, pw, ohd,
+    wsem, s1, r1, s2, r2, hs2, hr2, s3, r3, hs3, hr3, s4, r4, ws4, wr4,
 ):
     sp = lax.axis_index("space")
     me = lax.axis_index("chan")
@@ -88,11 +79,14 @@
     has_next = sp < n_space - 1
     fine = feat.shape[2]
     wide = fine // n_chan
-    parents = (SLAB_Y // 2) * (SLAB_Z // 2)
+    parents = dest_in.shape[1]
     cells = EDGE**3
     coarse_own = wd.shape[0]
     coarse = coarse_own * n_chan
     taps2 = 9
+    half = fine // coarse_own
+    crows = CLAYER // half
+    rows = LAYER // n_chan
 
     def rc(src, dst, ss, rs, space, chan):
         return pltpu.make_async_remote_copy(
@@ -104,12 +98,7 @@
             device_id_type=pl.DeviceIdType.MESH,
         )
 
-    copy_d = pltpu.make_async_copy(wd_hbm, wd, wsem.at[0])
-    copy_c = pltpu.make_async_copy(wc_hbm, wc, wsem.at[1])
-    copy_d.start()
-    copy_c.start()
     peers = [lax.rem(me + k, n_chan) for k in range(1, n_chan)]
-
     barrier = pltpu.get_barrier_semaphore()
 
     def greet(space, chan):
@@ -120,37 +109,40 @@
             device_id_type=pl.DeviceIdType.MESH,
         )
 
+    @pl.when(has_prev)
+    def _():
+        for chan in range(n_chan):
+            greet(sp - 1, chan)
+
+    @pl.when(has_next)
+    def _():
+        for chan in range(n_chan):
+            greet(sp + 1, chan)
+
     for chan in peers:
         greet(sp, chan)
 
-    @pl.when(has_prev)
-    def _():
-        for chan in range(n_chan):
-            greet(sp - 1, chan)
-
-    @pl.when(has_next)
-    def _():
-        for chan in range(n_chan):
-            greet(sp + 1, chan)
-
-    pl.semaphore_wait(
-        barrier, n_chan - 1 + n_chan * (has_prev.astype(jnp.int32) + has_next.astype(jnp.int32))
-    )
-
-    up_feat = rc(feat.at[:, pl.ds((EDGE - 1) * FACE, FACE), :], fh.at[0], s1.at[0, 0], r1.at[0, 0], sp + 1, me)
-    up_meta = rc(meta, mh.at[0], s1.at[0, 1], r1.at[0, 1], sp + 1, me)
-    dn_feat = rc(feat.at[:, pl.ds(0, FACE), :], fh.at[1], s1.at[1, 0], r1.at[1, 0], sp - 1, me)
-    dn_meta = rc(meta, mh.at[1], s1.at[1, 1], r1.at[1, 1], sp - 1, me)
-
-    @pl.when(has_next)
-    def _():
-        up_meta.start()
-        up_feat.start()
-
-    @pl.when(has_prev)
-    def _():
-        dn_meta.start()
-        dn_feat.start()
+    loads = [
+        pltpu.make_async_copy(src, dst, wsem.at[k])
+        for k, (src, dst) in enumerate(
+            (
+                (parent_hbm, parent_in),
+                (octant_hbm, octant_in),
+                (dest_hbm, dest_in),
+                (feat_hbm, feat),
+                (wf_hbm, wf),
+                (gain_hbm, gain),
+                (perm_h_hbm, perm_h),
+                (sel_d_hbm, sel_d),
+                (wd_hbm, wd),
+                (perm_c_hbm, perm_c),
+                (sel_c_hbm, sel_c),
+                (wc_hbm, wc),
+            )
+        )
+    ]
+    for load in loads:
+        load.start()
 
     @pl.when(jnp.logical_not(has_prev))
     def _():
@@ -169,11 +161,25 @@
         pb[2] = jnp.zeros(pb.shape[1:], BF)
         pw[2] = jnp.zeros(pw.shape[1:], F32)
 
+    blank_y = jnp.zeros((NX + 2, NZ, 3 * fine), BF)
+    s_buf[:, 0:NZ, :] = blank_y
+    s_buf[:, NZ + LAYER : 2 * NZ + LAYER, :] = blank_y
+
     lanes = meta.shape[1]
     columns = bricks * FACE
     spread = jnp.where(iota((lanes, columns), 1) // FACE == iota((lanes, columns), 0), 1.0, 0.0)
     face = iota((1, columns), 1) % FACE
     row_ids = iota((LAYER, columns), 0)
+
+    meta[...] = jnp.zeros(meta.shape, jnp.int32)
+    for load in loads[:4]:
+        load.wait()
+    local = parent_in[...] - sp * parents
+    octant = octant_in[...]
+    y_pos = 2 * (local // (SLAB_Z // 2)) + octant // 2 % 2
+    z_pos = 2 * (local % (SLAB_Z // 2)) + octant // 4
+    meta[0:1, 0:bricks] = octant % 2 + 2 * y_pos + 2 * SLAB_Y * z_pos
+    meta[1:2, 0:parents] = dest_in[...] - (sp - 1) * slots
 
     def keys_of(meta_block):
         code = jnp.dot(meta_block.astype(F32), spread, preferred_element_type=F32)[0:1].astype(jnp.int32)
@@ -188,10 +194,6 @@
         x_bit, y, z = key
         fits = (x_bit == x_want) & (z - c >= 0) & (z - c < NZ)
         return one(row_ids == jnp.where(fits, y * NZ + z - c, -1))
-
-    blank_y = jnp.zeros((NX + 2, NZ, 3 * fine), BF)
-    s_buf[:, 0:NZ, :] = blank_y
-    s_buf[:, NZ + LAYER : 2 * NZ + LAYER, :] = blank_y
 
     faces = jnp.concatenate(
         [feat[:, i * FACE : (i + 1) * FACE, :].reshape(columns, fine) for i in range(EDGE)], axis=1
@@ -215,14 +217,57 @@
                 parts.append(s_buf[x + 1 + a, (1 + b) * NZ : (1 + b) * NZ + LAYER, :])
         total = lax.dot_general(jnp.concatenate(parts, axis=1), wf[...], NT, preferred_element_type=F32)
         total = jnp.where(mask[x // EDGE][:, 0:wide] > 0.5, jnp.maximum(total, 0.0), 0.0)
-        rows = LAYER // n_chan
         packed = jnp.concatenate([total[j * rows : (j + 1) * rows] for j in range(n_chan)], axis=1)
         g_buf[x + 1, me] = packed.astype(BF)
+
+    def send_layer(x):
         for k, chan in enumerate(peers):
             rc(g_buf.at[x + 1, me], g_buf.at[x + 1, me], s2.at[x, k], r2.at[x, me], sp, chan).start()
 
-    for x in range(1, NX - 1):
+    early = NX // 2
+    for load in loads[4:6]:
+        load.wait()
+    for x in range(1, early):
         hidden_layer(x)
+
+    pl.semaphore_wait(
+        barrier, n_chan - 1 + n_chan * (has_prev.astype(jnp.int32) + has_next.astype(jnp.int32))
+    )
+
+    up_feat = rc(feat.at[:, pl.ds((EDGE - 1) * FACE, FACE), :], fh.at[0], s1.at[0, 0], r1.at[0, 0], sp + 1, me)
+    up_meta = rc(meta, mh.at[0], s1.at[0, 1], r1.at[0, 1], sp + 1, me)
+    dn_feat = rc(feat.at[:, pl.ds(0, FACE), :], fh.at[1], s1.at[1, 0], r1.at[1, 0], sp - 1, me)
+    dn_meta = rc(meta, mh.at[1], s1.at[1, 1], r1.at[1, 1], sp - 1, me)
+
+    @pl.when(has_next)
+    def _():
+        up_meta.start()
+        up_feat.start()
+
+    @pl.when(has_prev)
+    def _():
+        dn_meta.start()
+        dn_feat.start()
+
+    for x in range(1, early):
+        send_layer(x)
+    for x in range(early, NX - 1):
+        hidden_layer(x)
+        send_layer(x)
+
+    lane_par = jnp.where(
+        iota((lanes, parents * cells), 1) // cells == iota((lanes, parents * cells), 0), 1.0, 0.0
+    )
+
+    def dest_table(k):
+        block = meta[...] if k == 1 else mh[k // 2]
+        rel = jnp.dot(block.astype(F32), lane_par, preferred_element_type=F32)[1:2].astype(jnp.int32)
+        slot = rel - (2 - k) * slots
+        target = slot * cells + iota((1, parents * cells), 1) % cells
+        ids = iota((slots * cells, parents * cells), 0)
+        ohd[k] = one(ids == jnp.where((slot >= 0) & (slot < slots), target, -1))
+
+    dest_table(1)
 
     def halo_layer(side):
         k = keys_of(mh[side])
@@ -245,6 +290,8 @@
         for chan in range(n_chan):
             rc(g_buf.at[NX, me], g_buf.at[0, me], hs2.at[chan], hr2.at[me], sp + 1, chan).start()
 
+    send_layer(NX - 1)
+
     @pl.when(has_prev)
     def _():
         up_meta.wait_recv()
@@ -252,83 +299,71 @@
 
     halo_layer(0)
     hidden_layer(0)
-
-    big = n_chan * fine
-    r, q = iota((big, big), 0), iota((big, big), 1)
-    perm_h[...] = one((r % fine) // wide * fine + r // fine * wide + r % wide == q)
-    half = fine // coarse_own
-    big2 = n_chan * fine
-    perm_c[...] = one((r % fine) // coarse_own * coarse + r // fine * coarse_own + r % coarse_own == q)
-    del big2
-
-    r, q = iota((taps2 * CLAYER, LAYER), 0), iota((taps2 * CLAYER, LAYER), 1)
-    bc, at = r // CLAYER, r % CLAYER
-    y = 2 * (at // CZ) + bc // 3 - 1
-    z = 2 * (at % CZ) + bc % 3 - 1
-    sel_d[...] = one((y >= 0) & (z >= 0) & (y * NZ + z == q))
-    r, q = iota((taps2 * CLAYER, CLAYER), 0), iota((taps2 * CLAYER, CLAYER), 1)
-    bc, at = r // CLAYER, r % CLAYER
-    par, yz = at // FACE, at % FACE
-    y = par // (SLAB_Z // 2) * EDGE + yz // EDGE + bc // 3 - 1
-    z = par % (SLAB_Z // 2) * EDGE + yz % EDGE + bc % 3 - 1
-    sel_c[...] = one((y >= 0) & (z >= 0) & (z < CZ) & (y * CZ + z == q))
-
-    lane_par = jnp.where(
-        iota((lanes, parents * cells), 1) // cells == iota((lanes, parents * cells), 0), 1.0, 0.0
-    )
-    out_ids = iota((slots * cells, parents * cells), 0)
-    for k in range(3):
-        block = meta[...] if k == 1 else mh[k // 2]
-        rel = jnp.dot(block.astype(F32), lane_par, preferred_element_type=F32)[1:2].astype(jnp.int32)
-        slot = rel - (2 - k) * slots
-        target = slot * cells + iota((1, parents * cells), 1) % cells
-        ohd[k] = one(out_ids == jnp.where((slot >= 0) & (slot < slots), target, -1))
-
-    for x in range(NX):
+    send_layer(0)
+
+    def wait_layer(x):
         for k in range(1, n_chan):
             src = lax.rem(me + k, n_chan)
             rc(g_buf.at[x + 1, src], g_buf.at[x + 1, src], s2.at[x, 0], r2.at[x, src], sp, src).wait_recv()
 
+    def spread_layers(buf, at, perm, height, width, parts):
+        gathered = jnp.concatenate(
+            [jnp.concatenate([buf[x, s] for s in range(n_chan)], axis=1) for x in at], axis=0
+        )
+        moved = pick(gathered, perm[...]).astype(BF)
+        layers = [
+            jnp.concatenate(
+                [moved[i * height : (i + 1) * height, j * width : (j + 1) * width] for j in range(parts)],
+                axis=0,
+            )
+            for i in range(len(at))
+        ]
+        return jnp.concatenate(layers, axis=1)
+
+    def fill_d(at):
+        filled = pick(sel_d[...], spread_layers(g_buf, at, perm_h, rows, fine, n_chan)).astype(BF)
+        for i, x in enumerate(at):
+            d_buf[:, x * fine : (x + 1) * fine] = filled[:, i * fine : (i + 1) * fine]
+
+    def down(at):
+        stacked = []
+        for x in at:
+            stacked.append(
+                jnp.concatenate(
+                    [
+                        d_buf[bc * CLAYER : (bc + 1) * CLAYER, (2 * x + a) * fine : (2 * x + a + 1) * fine]
+                        for a in range(3)
+                        for bc in range(taps2)
+                    ],
+                    axis=1,
+                )
+            )
+        pieces = lax.dot_general(jnp.concatenate(stacked, axis=0), wd[...], NT, preferred_element_type=F32)
+        for i, x in enumerate(at):
+            live = pick(sel_d[4 * CLAYER : 5 * CLAYER, :], mask[x // 2].astype(BF))[:, 0:coarse_own]
+            part = pieces[i * CLAYER : (i + 1) * CLAYER]
+            part = jnp.where(live > 0.5, jnp.maximum(part, 0.0), 0.0)
+            c_buf[x + 1, me] = jnp.concatenate(
+                [part[j * crows : (j + 1) * crows] for j in range(half)], axis=1
+            ).astype(BF)
+
+    inner = list(range(1, CX - 1))
+    for load in loads[6:9]:
+        load.wait()
+    for x in range(1, NX - 1):
+        wait_layer(x)
+    fill_d(list(range(2, NX)))
+    down(inner)
+
     @pl.when(has_prev)
     def _():
         for chan in range(n_chan):
             rc(g_buf.at[0, chan], g_buf.at[0, chan], hs2.at[chan], hr2.at[chan], sp - 1, chan).wait_recv()
 
-    gathered = jnp.concatenate(
-        [jnp.concatenate([g_buf[x, s] for s in range(n_chan)], axis=1) for x in range(NX + 1)], axis=0
-    )
-    rows = LAYER // n_chan
-    spread_h = pick(gathered, perm_h[...]).astype(BF)
-    layers = [
-        jnp.concatenate(
-            [spread_h[x * rows : (x + 1) * rows, j * fine : (j + 1) * fine] for j in range(n_chan)], axis=0
-        )
-        for x in range(NX + 1)
-    ]
-    d_buf[...] = pick(sel_d[...], jnp.concatenate(layers, axis=1)).astype(BF)
-
-    copy_d.wait()
-    stacked = []
-    for x in range(CX):
-        stacked.append(
-            jnp.concatenate(
-                [
-                    d_buf[bc * CLAYER : (bc + 1) * CLAYER, (2 * x + a) * fine : (2 * x + a + 1) * fine]
-                    for a in range(3)
-                    for bc in range(taps2)
-                ],
-                axis=1,
-            )
-        )
-    pieces = lax.dot_general(jnp.concatenate(stacked, axis=0), wd[...], NT, preferred_element_type=F32)
-    crows = CLAYER // half
-    for x in range(CX):
-        live = pick(sel_d[4 * CLAYER : 5 * CLAYER, :], mask[x // 2].astype(BF))[:, 0:coarse_own]
-        part = pieces[x * CLAYER : (x + 1) * CLAYER]
-        part = jnp.where(live > 0.5, jnp.maximum(part, 0.0), 0.0)
-        c_buf[x + 1, me] = jnp.concatenate(
-            [part[j * crows : (j + 1) * crows] for j in range(half)], axis=1
-        ).astype(BF)
+    wait_layer(NX - 1)
+    wait_layer(0)
+    fill_d([0, 1, NX])
+    down([0, CX - 1])
 
     @pl.when(has_next)
     def _():
@@ -343,37 +378,23 @@
     own_c = c_buf.at[pl.ds(1, CX), me]
     for k, chan in enumerate(peers):
         rc(own_c, own_c, s3.at[k], r3.at[me], sp, chan).start()
+
+    dest_table(0)
+    dest_table(2)
+    for load in loads[9:]:
+        load.wait()
+
     for k in range(1, n_chan):
         src = lax.rem(me + k, n_chan)
         ref = c_buf.at[pl.ds(1, CX), src]
         rc(ref, ref, s3.at[0], r3.at[src], sp, src).wait_recv()
 
-    @pl.when(has_prev)
-    def _():
-        for chan in range(n_chan):
-            ref = c_buf.at[0, chan]
-            rc(ref, ref, hs3.at[0, chan], hr3.at[0, chan], sp - 1, chan).wait_recv()
-
-    @pl.when(has_next)
-    def _():
-        for chan in range(n_chan):
-            ref = c_buf.at[CX + 1, chan]
-            rc(ref, ref, hs3.at[1, chan], hr3.at[1, chan], sp + 1, chan).wait_recv()
-
-    gathered = jnp.concatenate(
-        [jnp.concatenate([c_buf[x, s] for s in range(n_chan)], axis=1) for x in range(CX + 2)], axis=0
-    )
-    spread_c = pick(gathered, perm_c[...]).astype(BF)
-    layers = [
-        jnp.concatenate(
-            [spread_c[x * crows : (x + 1) * crows, j * coarse : (j + 1) * coarse] for j in range(half)], axis=0
-        )
-        for x in range(CX + 2)
-    ]
-    e_buf[...] = pick(sel_c[...], jnp.concatenate(layers, axis=1)).astype(BF)
-    copy_c.wait()
-    total = None
-    for a in range(3):
+    def fill_e(at):
+        filled = pick(sel_c[...], spread_layers(c_buf, at, perm_c, crows, coarse, half)).astype(BF)
+        for i, x in enumerate(at):
+            e_buf[:, x * coarse : (x + 1) * coarse] = filled[:, i * coarse : (i + 1) * coarse]
+
+    def coarse_taps(a, total):
         for bc in range(taps2):
             block = jnp.concatenate(
                 [
@@ -389,6 +410,26 @@
             t = a * taps2 + bc
             term = lax.dot_general(wc[:, t * coarse : (t + 1) * coarse], block, NT, preferred_element_type=F32)
             total = term if total is None else total + term
+        return total
+
+    fill_e(list(range(1, CX + 1)))
+    total = coarse_taps(1, None)
+
+    @pl.when(has_prev)
+    def _():
+        for chan in range(n_chan):
+            ref = c_buf.at[0, chan]
+            rc(ref, ref, hs3.at[0, chan], hr3.at[0, chan], sp - 1, chan).wait_recv()
+
+    @pl.when(has_next)
+    def _():
+        for chan in range(n_chan):
+            ref = c_buf.at[CX + 1, chan]
+            rc(ref, ref, hs3.at[1, chan], hr3.at[1, chan], sp + 1, chan).wait_recv()
+
+    fill_e([0, CX + 1])
+    total = coarse_taps(0, total)
+    total = coarse_taps(2, total)
     rounded = total.astype(BF)
     pb[1] = rounded
     values = rounded.astype(F32)
@@ -468,33 +509,31 @@
 
 
 def body(n_space, n_chan, features, neighbours, parent_index, octant, parent_dest, conv_fine, conv_down, conv_coarse, norm_gain):
-    device = lax.axis_index("space")
     bricks, _, fine = features.shape
     parents = parent_dest.shape[0]
     slots = 2 * parents
-    local = parent_index - device * parents
-    y_pos = 2 * (local // (SLAB_Z // 2)) + octant // 2 % 2
-    z_pos = 2 * (local % (SLAB_Z // 2)) + octant // 4
-    code = octant % 2 + 2 * y_pos + 2 * SLAB_Y * z_pos
-    rel = parent_dest - (device - 1) * slots
-    meta = jnp.concatenate(
-        [jnp.pad(code, (0, 128 - bricks))[None], jnp.pad(rel, (0, 128 - parents))[None], jnp.zeros((6, 128), jnp.int32)], 0
-    )
     down = conv_down.shape[0]
     own = conv_coarse.shape[0]
     cells = EDGE**3
     coarse = down * n_chan
     vmem = pl.BlockSpec(memory_space=pltpu.VMEM)
-    hbm = pl.BlockSpec(memory_space=pl.ANY)
+    hbm = pl.BlockSpec(memory_space=pltpu.HBM)
     dma = pltpu.SemaphoreType.DMA
     big = n_chan * fine
     crows = CLAYER // (fine // down)
     return pl.pallas_call(
         functools.partial(fused_kernel, n_space, n_chan, bricks, slots),
         out_shape=jax.ShapeDtypeStruct((own, slots * cells), BF),
-        in_specs=[vmem, vmem, vmem, hbm, hbm, vmem],
+        in_specs=[hbm] * 12,
         out_specs=vmem,
         scratch_shapes=[
+            pltpu.VMEM(features.shape, BF),
+            pltpu.VMEM(conv_fine.shape, BF),
+            pltpu.VMEM((1, own), F32),
+            pltpu.VMEM((1, bricks), jnp.int32),
+            pltpu.VMEM((1, bricks), jnp.int32),
+            pltpu.VMEM((1, parents), jnp.int32),
+            pltpu.VMEM((8, 128), jnp.int32),
             pltpu.VMEM(conv_down.shape, BF),
             pltpu.VMEM(conv_coarse.shape, BF),
             pltpu.VMEM((2, bricks, FACE, fine), BF),
@@ -512,7 +551,7 @@
             pltpu.VMEM((3, own, parents * cells), BF),
             pltpu.VMEM((3, n_chan, 1, parents * cells), F32),
             pltpu.VMEM((3, slots * cells, parents * cells), BF),
-            dma((2,)),
+            dma((12,)),
             dma((2, 2)),
             dma((2, 2)),
             dma((NX, n_chan - 1)),
@@ -528,8 +567,19 @@
             dma((3, n_chan)),
             dma((3, n_chan)),
         ],
-        compiler_params=pltpu.CompilerParams(collective_id=0, has_side_effects=True),
-    )(features, meta, conv_fine, conv_down, conv_coarse, norm_gain.reshape(1, -1))
+        compiler_params=pltpu.CompilerParams(collective_id=0, has_side_effects=True, vmem_limit_bytes=66900000
+        ),
+    )(
+        features,
+        parent_index.reshape(1, -1),
+        octant.reshape(1, -1),
+        parent_dest.reshape(1, -1),
+        conv_fine,
+        conv_down,
+        conv_coarse,
+        norm_gain.reshape(1, -1),
+        *tables(n_chan, fine, down),
+    )
 
 
 def solution(mesh):

time: 36.5 us -> 31.1 us (0.85)
  Pallas kernels: 32.7 us -> 29.1 us
  local copies, waits for them, and re-layouts: 2.88 us -> 1.47 us
  other arithmetic: 0.69 us -> 0 us
    pallas_call x1, Pallas kernels: 32.7 us -> 29.1 us  [body(): pl.pallas_call(functools.partial(fused_kernel, n_space, n_chan, bricks, s...]
    unnamed x7 -> x1, local copies, waits for them, and re-layouts: 2.79 us -> 1.47 us
    concatenate x1 -> x0, other arithmetic: 0.67 us -> none  [body(): jnp.concatenate([jnp.pad(code, (0, 128 - bricks))[None], jnp.pad(rel, (0,...]
where the time goes in v2:
time: 31.1 us; the launch traced here: 30.6 us
  Pallas kernels  29.1 us (94%)
  local copies, waits for them, and re-layouts  1.47 us (5%)
    pallas_call x1, Pallas kernels, body(): pl.pallas_call(functools.partial(fused_kernel, n_space, n_chan, bricks, s...  29.1 us
    unnamed x1, local copies, waits for them, and re-layouts  1.47 us

profile of v2, /device:TPU:0, one launch (start us, length us, event | category | flops | bytes accessed | tf_op | source)
XLA Modules:
  0.0 30.6 jit_solution(12383260367099543921)
XLA Ops:
  0.0 29.1 %shard_map.118 = bf16[64,512]{1,0:T(8,128)(2,1)} custom-call(bf16[16,64,128]{2,1,0:T(8,128)(2,1)} %feat_hbm.1, s32[1,16]{1,0:T(1,128)} %bitcast.4, s32[1,16]{1,0:T(1,128)} %bitcast.5, s32[1,4]{1,0:T(1,128)} %bitcast.6, bf16[32,3456]{1,0:T(8,128)(2,1)} %wf_hbm.1, bf16[64,3456]{1,0:T(8,128)(2,1)} %wd_hbm.1, bf16[64,6912]{1,0:T(8,128)(2,1)} %wc_hbm.1, ...), custom_call_target="tpu_custom_call" | custom-call | tf_op jit(solution)/shard_map/pallas_call | solution.py:524
  29.1 1.5 %copy.14 = bf16[64,512]{1,0:T(8,128)(2,1)} copy(bf16[64,512]{1,0:T(8,128)(2,1)} %shard_map.118) | data formatting | bytes 131072

commit v3 on v2

--- a/solution.py
+++ b/solution.py
@@ -70,7 +70,7 @@
     perm_h_hbm, perm_c_hbm, sel_d_hbm, sel_c_hbm,
     out,
     feat, wf, gain, parent_in, octant_in, dest_in, meta, wd, wc, fh, mh, s_buf, mask, g_buf,
-    perm_h, perm_c, sel_d, sel_c, d_buf, c_buf, e_buf, pb, pw, ohd,
+    perm_h, perm_c, sel_d, sel_c, d_buf, c_buf, e_buf, pb, pw, ohd, hot0, hot_t, sel_x,
     wsem, s1, r1, s2, r2, hs2, hr2, s3, r3, hs3, hr3, s4, r4, ws4, wr4,
 ):
     sp = lax.axis_index("space")
@@ -86,7 +86,7 @@
     taps2 = 9
     half = fine // coarse_own
     crows = CLAYER // half
-    rows = LAYER // n_chan
+    rows = bricks * FACE // n_chan
 
     def rc(src, dst, ss, rs, space, chan):
         return pltpu.make_async_remote_copy(
@@ -209,6 +209,8 @@
                 ]
             if c == 0:
                 mask[x] = pick(hot, jnp.ones((columns, fine), BF))
+                hot0[x] = hot
+                hot_t[:, x * LAYER : (x + 1) * LAYER] = hot.astype(F32).T.astype(BF)
 
     def hidden_layer(x):
         parts = []
@@ -216,19 +218,21 @@
             for b in (-1, 0, 1):
                 parts.append(s_buf[x + 1 + a, (1 + b) * NZ : (1 + b) * NZ + LAYER, :])
         total = lax.dot_general(jnp.concatenate(parts, axis=1), wf[...], NT, preferred_element_type=F32)
-        total = jnp.where(mask[x // EDGE][:, 0:wide] > 0.5, jnp.maximum(total, 0.0), 0.0)
+        return jnp.maximum(total, 0.0).astype(BF)
+
+    def pack(i, low, high):
+        total = pick(hot_t[...], jnp.concatenate([low, high], axis=0))
         packed = jnp.concatenate([total[j * rows : (j + 1) * rows] for j in range(n_chan)], axis=1)
-        g_buf[x + 1, me] = packed.astype(BF)
-
-    def send_layer(x):
+        g_buf[i + 1, me] = packed.astype(BF)
+
+    def send_layer(i):
         for k, chan in enumerate(peers):
-            rc(g_buf.at[x + 1, me], g_buf.at[x + 1, me], s2.at[x, k], r2.at[x, me], sp, chan).start()
-
-    early = NX // 2
+            rc(g_buf.at[i + 1, me], g_buf.at[i + 1, me], s2.at[i, k], r2.at[i, me], sp, chan).start()
+
     for load in loads[4:6]:
         load.wait()
-    for x in range(1, early):
-        hidden_layer(x)
+    pack(1, hidden_layer(1), hidden_layer(EDGE + 1))
+    early = hidden_layer(2)
 
     pl.semaphore_wait(
         barrier, n_chan - 1 + n_chan * (has_prev.astype(jnp.int32) + has_next.astype(jnp.int32))
@@ -249,11 +253,11 @@
         dn_meta.start()
         dn_feat.start()
 
-    for x in range(1, early):
-        send_layer(x)
-    for x in range(early, NX - 1):
-        hidden_layer(x)
-        send_layer(x)
+    send_layer(1)
+    pack(2, early, hidden_layer(EDGE + 2))
+    send_layer(2)
+    third = hidden_layer(EDGE - 1)
+    fourth = hidden_layer(EDGE)
 
     lane_par = jnp.where(
         iota((lanes, parents * cells), 1) // cells == iota((lanes, parents * cells), 0), 1.0, 0.0
@@ -268,14 +272,21 @@
         ohd[k] = one(ids == jnp.where((slot >= 0) & (slot < slots), target, -1))
 
     dest_table(1)
+    for load in loads[6:9]:
+        load.wait()
+    for x in range(2):
+        sel_x[x] = pick(sel_d[...], hot0[x]).astype(BF)
 
     def halo_layer(side):
         k = keys_of(mh[side])
         block = fh[side].reshape(columns, fine)
         for c in (-1, 0, 1):
+            hot = one_hot(k, 1 - side, c)
             s_buf[0 if side == 0 else NX + 1, NZ : NZ + LAYER, (c + 1) * fine : (c + 2) * fine] = pick(
-                one_hot(k, 1 - side, c), block
+                hot, block
             ).astype(BF)
+            if side == 0 and c == 0:
+                sel_x[2] = pick(sel_d[...], hot).astype(BF)
 
     @pl.when(has_next)
     def _():
@@ -283,14 +294,14 @@
         dn_feat.wait_recv()
 
     halo_layer(1)
-    hidden_layer(NX - 1)
-
-    @pl.when(has_next)
-    def _():
-        for chan in range(n_chan):
-            rc(g_buf.at[NX, me], g_buf.at[0, me], hs2.at[chan], hr2.at[me], sp + 1, chan).start()
-
-    send_layer(NX - 1)
+    pack(EDGE - 1, third, hidden_layer(NX - 1))
+
+    @pl.when(has_next)
+    def _():
+        for chan in range(n_chan):
+            rc(g_buf.at[EDGE, me], g_buf.at[0, me], hs2.at[chan], hr2.at[me], sp + 1, chan).start()
+
+    send_layer(EDGE - 1)
 
     @pl.when(has_prev)
     def _():
@@ -298,7 +309,7 @@
         up_feat.wait_recv()
 
     halo_layer(0)
-    hidden_layer(0)
+    pack(0, hidden_layer(0), fourth)
     send_layer(0)
 
     def wait_layer(x):
@@ -321,9 +332,17 @@
         return jnp.concatenate(layers, axis=1)
 
     def fill_d(at):
-        filled = pick(sel_d[...], spread_layers(g_buf, at, perm_h, rows, fine, n_chan)).astype(BF)
-        for i, x in enumerate(at):
-            d_buf[:, x * fine : (x + 1) * fine] = filled[:, i * fine : (i + 1) * fine]
+        moved = spread_layers(g_buf, [i + 1 for i in at], perm_h, rows, fine, n_chan)
+        owned = [k for k, i in enumerate(at) if i >= 0]
+        for x in range(3):
+            kept = owned if x < 2 else [k for k, i in enumerate(at) if i < 0]
+            if not kept:
+                continue
+            block = jnp.concatenate([moved[:, k * fine : (k + 1) * fine] for k in kept], axis=1)
+            filled = pick(sel_x[x], block).astype(BF)
+            for n, k in enumerate(kept):
+                at_x = 1 + EDGE * x + at[k] if x < 2 else 0
+                d_buf[:, at_x * fine : (at_x + 1) * fine] = filled[:, n * fine : (n + 1) * fine]
 
     def down(at):
         stacked = []
@@ -347,23 +366,19 @@
                 [part[j * crows : (j + 1) * crows] for j in range(half)], axis=1
             ).astype(BF)
 
-    inner = list(range(1, CX - 1))
-    for load in loads[6:9]:
-        load.wait()
-    for x in range(1, NX - 1):
-        wait_layer(x)
-    fill_d(list(range(2, NX)))
-    down(inner)
+    wait_layer(1)
+    wait_layer(2)
+    fill_d([1, 2])
 
     @pl.when(has_prev)
     def _():
         for chan in range(n_chan):
             rc(g_buf.at[0, chan], g_buf.at[0, chan], hs2.at[chan], hr2.at[chan], sp - 1, chan).wait_recv()
 
-    wait_layer(NX - 1)
+    wait_layer(EDGE - 1)
     wait_layer(0)
-    fill_d([0, 1, NX])
-    down([0, CX - 1])
+    fill_d([-1, 0, EDGE - 1])
+    down(range(CX))
 
     @pl.when(has_next)
     def _():
@@ -481,7 +496,7 @@
 
     out[...] = (result + normed(0) + normed(2)).astype(BF)
 
-    for x in range(NX):
+    for x in range(EDGE):
         for k, chan in enumerate(peers):
             rc(g_buf.at[x + 1, me], g_buf.at[x + 1, me], s2.at[x, k], r2.at[x, me], sp, chan).wait_send()
     for k, chan in enumerate(peers):
@@ -494,7 +509,7 @@
         up_feat.wait_send()
         rc(pb.at[1], pb.at[0], s4.at[0], r4.at[0], sp + 1, me).wait_send()
         for chan in range(n_chan):
-            rc(g_buf.at[NX, me], g_buf.at[0, me], hs2.at[chan], hr2.at[me], sp + 1, chan).wait_send()
+            rc(g_buf.at[EDGE, me], g_buf.at[0, me], hs2.at[chan], hr2.at[me], sp + 1, chan).wait_send()
             rc(c_buf.at[CX, me], c_buf.at[0, me], hs3.at[0, chan], hr3.at[0, me], sp + 1, chan).wait_send()
             rc(pw.at[1, me], pw.at[0, me], ws4.at[0, chan], wr4.at[0, me], sp + 1, chan).wait_send()
 
@@ -540,7 +555,7 @@
             pltpu.VMEM((2, 8, 128), jnp.int32),
             pltpu.VMEM((NX + 2, LAYER + 2 * NZ, 3 * fine), BF),
             pltpu.VMEM((2, LAYER, fine), F32),
-            pltpu.VMEM((NX + 1, n_chan, LAYER // n_chan, fine), BF),
+            pltpu.VMEM((EDGE + 1, n_chan, bricks * FACE // n_chan, fine), BF),
             pltpu.VMEM((big, big), BF),
             pltpu.VMEM((big, big), BF),
             pltpu.VMEM((9 * CLAYER, LAYER), BF),
@@ -551,11 +566,14 @@
             pltpu.VMEM((3, own, parents * cells), BF),
             pltpu.VMEM((3, n_chan, 1, parents * cells), F32),
             pltpu.VMEM((3, slots * cells, parents * cells), BF),
+            pltpu.VMEM((2, LAYER, bricks * FACE), BF),
+            pltpu.VMEM((bricks * FACE, 2 * LAYER), BF),
+            pltpu.VMEM((3, 9 * CLAYER, bricks * FACE), BF),
             dma((12,)),
             dma((2, 2)),
             dma((2, 2)),
-            dma((NX, n_chan - 1)),
-            dma((NX, n_chan)),
+            dma((EDGE, n_chan - 1)),
+            dma((EDGE, n_chan)),
             dma((n_chan,)),
             dma((n_chan,)),
             dma((n_chan - 1,)),

time: 31.1 us -> 31.8 us (1.023)
  Pallas kernels: 29.1 us -> 29.8 us
    pallas_call x1, Pallas kernels: 29.1 us -> 29.8 us  [body(): pl.pallas_call(functools.partial(fused_kernel, n_space, n_chan, bricks, s...]
where the time goes in v3:
time: 31.8 us; the launch traced here: 31.3 us
  Pallas kernels  29.8 us (94%)
  local copies, waits for them, and re-layouts  1.47 us (5%)
    pallas_call x1, Pallas kernels, body(): pl.pallas_call(functools.partial(fused_kernel, n_space, n_chan, bricks, s...  29.8 us
    unnamed x1, local copies, waits for them, and re-layouts  1.47 us

profile of v3, /device:TPU:0, one launch (start us, length us, event | category | flops | bytes accessed | tf_op | source)
XLA Modules:
  0.0 31.3 jit_solution(15660359210536912484)
XLA Ops:
  0.0 29.8 %shard_map.118 = bf16[64,512]{1,0:T(8,128)(2,1)} custom-call(bf16[16,64,128]{2,1,0:T(8,128)(2,1)} %feat_hbm.1, s32[1,16]{1,0:T(1,128)} %bitcast.4, s32[1,16]{1,0:T(1,128)} %bitcast.5, s32[1,4]{1,0:T(1,128)} %bitcast.6, bf16[32,3456]{1,0:T(8,128)(2,1)} %wf_hbm.1, bf16[64,3456]{1,0:T(8,128)(2,1)} %wd_hbm.1, bf16[64,6912]{1,0:T(8,128)(2,1)} %wc_hbm.1, ...), custom_call_target="tpu_custom_call" | custom-call | tf_op jit(solution)/shard_map/pallas_call | solution.py:539
  29.8 1.5 %copy.14 = bf16[64,512]{1,0:T(8,128)(2,1)} copy(bf16[64,512]{1,0:T(8,128)(2,1)} %shard_map.118) | data formatting | bytes 131072
